TPU v7x, 256 devices: a whole 4x4x8 slice. The times are simulated.
256 devices in a mesh: segment: 4 (over z_hi, core), dp: 16 (over z_lo, y), mp: 4 (over x).
Axes of the slice: x: 4, y: 4, z: 8 (z_hi: 2, z_lo: 4; z = z_hi * 4 + z_lo), core: 2. Of those that a mesh axis runs over, the one named last changes fastest.
Arguments:
- hidden: bfloat16 [384, 64, 4096], P(('segment', 'dp'))
- final_gain: bfloat16 [4096], replicated, may hold values from 0.099609375 to 1.8984375
- key_weight: bfloat16 [4096, 2048], P('dp', 'mp'), may hold values from -0.09375 to 0.09375
- value_weight: bfloat16 [4096, 2048], P('dp', 'mp'), may hold values from -0.09375 to 0.09375
- queries: bfloat16 [32, 128, 2048], P('dp', None, 'mp'), may hold values from -6 to 6
- context_grad: bfloat16 [32, 128, 2048], P('dp', None, 'mp'), may hold values from -384 to 384
- passage_count: int32 [32], replicated, may hold values from 4 to 16, as said below
- passage_slot: int32 [32, 16], replicated, may hold values from -1 to 287, as said below
- slot_question: int32 [32], replicated, may hold values from 0 to 31, as said below
Outputs:
- grad_hidden: bfloat16 [384, 64, 4096], P(('segment', 'dp'), 'mp')
Inputs may be any that keep to these rules, and one draw needn't show every extreme that they name: `passage_count`: the counts add up to 288, and some question has 16 passages. `passage_slot`: entry [q, j] is the slot holding passage j of question q for j below passage_count[q], and -1 beyond. Slots are numbered device by device in the order of the segment and dp indices, 6 to a device; only devices of the first three segment indices hold passages, each of their slots exactly one, and no slot is named twice. One device holds at most 1 passages of the questions served by the decoder rows of one dp index (rows 2 * c to 2 * c + 1 on dp index c), and one segment index at most 6 passages of one question; both bounds are reached. `slot_question`: A permutation.
All inputs are finite; a program needn't handle non-finite values.
Results may differ from a plain program's by a relative error of at most 0.015.
Values may be sent and summed in bfloat16 or wider, within the bound.
A program may use at most 128 MiB of HBM per device.

v0:
```python
import math
import jax
import jax.numpy as jnp
from jax import lax
from jax.sharding import PartitionSpec as P

HEAD_DIM = 64
EPSILON = 1e-06


def on_device(
    hidden,
    final_gain,
    key_weight,
    value_weight,
    queries,
    context_grad,
    passage_count,
    passage_slot,
    slot_question,
):
    segments = lax.axis_size("segment")
    columns = lax.axis_size("dp")
    tensor_ways = lax.axis_size("mp")
    segment_at = lax.axis_index("segment")
    column_at = lax.axis_index("dp")
    tensor_at = lax.axis_index("mp")
    slots_here = hidden.shape[0]
    seq_len = hidden.shape[1]
    model_width = hidden.shape[2]
    questions = passage_count.shape[0]
    most_passages = passage_slot.shape[1]
    q_here = queries.shape[0]
    target_len = queries.shape[1]
    encoders = (segments - 1) * columns
    per_device = (q_here * most_passages + encoders - 1) // encoders
    per_segment = (most_passages + segments - 2) // (segments - 1)
    inner_here = key_weight.shape[1]
    heads_here = inner_here // HEAD_DIM
    row_count = slots_here * seq_len
    scaling = 1.0 / math.sqrt(HEAD_DIM)
    key_full, value_full = (
        lax.all_gather(key_weight, "dp", axis=0, tiled=True),
        lax.all_gather(value_weight, "dp", axis=0, tiled=True),
    )

    def project(normed_rows, weight_full):
        return jnp.dot(normed_rows, weight_full, preferred_element_type=jnp.float32)

    def project_back(grad_rows, weight_full):
        return lax.dot_general(
            grad_rows, weight_full, (((1,), (1,)), ((), ())), preferred_element_type=jnp.float32
        )

    hidden_rows = hidden.reshape(row_count, model_width)
    gain_vec = final_gain.astype(jnp.float32)
    inv_rms = lax.rsqrt(
        jnp.mean(jnp.square(hidden_rows.astype(jnp.float32)), axis=-1, keepdims=True) + EPSILON
    )
    normed = (hidden_rows.astype(jnp.float32) * inv_rms * gain_vec).astype(jnp.bfloat16)
    key_rows = project(normed, key_full).astype(jnp.bfloat16)
    value_rows = project(normed, value_full).astype(jnp.bfloat16)
    packed = jnp.concatenate([key_rows, value_rows], axis=-1).reshape(
        slots_here, seq_len, 2 * inner_here
    )
    question_ids = jnp.arange(questions, dtype=jnp.int32)
    passage_ids = jnp.arange(most_passages, dtype=jnp.int32)
    home_row = jnp.sum(
        jnp.where(slot_question[None, :] == question_ids[:, None], question_ids[None, :], 0), axis=1
    )
    present = (passage_slot >= 0) & (passage_ids[None, :] < passage_count[:, None])
    local_ids = jnp.arange(slots_here, dtype=jnp.int32)
    my_slots = (segment_at * columns + column_at) * slots_here + local_ids
    matched = (passage_slot[None, :, :] == my_slots[:, None, None]) & present[None, :, :]
    holding = jnp.any(matched, axis=(1, 2))
    owner_question = jnp.sum(jnp.where(matched, question_ids[None, :, None], 0), axis=(1, 2))
    owner_row = jnp.sum(
        jnp.where(owner_question[:, None] == question_ids[None, :], home_row[None, :], 0), axis=1
    )
    target_column = owner_row // q_here
    earlier = (
        holding[None, :]
        & (target_column[None, :] == target_column[:, None])
        & (local_ids[None, :] < local_ids[:, None])
    )
    send_rank = jnp.sum(earlier.astype(jnp.int32), axis=1)
    send_pick = (
        holding[None, None, :]
        & (target_column[None, None, :] == jnp.arange(columns, dtype=jnp.int32)[:, None, None])
        & (send_rank[None, None, :] == jnp.arange(per_device, dtype=jnp.int32)[None, :, None])
    ).astype(jnp.bfloat16)
    outgoing = jnp.einsum(
        "gcl,lsx->gcsx", send_pick, packed, preferred_element_type=jnp.float32
    ).astype(jnp.bfloat16)
    incoming = lax.all_to_all(outgoing, "dp", split_axis=0, concat_axis=0, tiled=True)
    row_ids = column_at * q_here + jnp.arange(q_here, dtype=jnp.int32)
    my_questions = jnp.sum(
        jnp.where(row_ids[:, None] == question_ids[None, :], slot_question[None, :], 0), axis=1
    )
    is_mine = my_questions[:, None] == question_ids[None, :]
    row_slots = jnp.sum(
        jnp.where(is_mine[:, :, None], passage_slot[None, :, :], 0), axis=1
    ).reshape(-1)
    row_live = jnp.any(is_mine[:, :, None] & present[None, :, :], axis=1).reshape(-1)
    question_of = jnp.repeat(jnp.arange(q_here, dtype=jnp.int32), most_passages)
    segment_slots = columns * slots_here
    segment_of = row_slots // segment_slots
    column_key = row_slots % segment_slots
    source_of = column_key // slots_here
    on_segment = row_live & (segment_of == segment_at)
    ahead = on_segment[None, :] & (column_key[None, :] < column_key[:, None])
    segment_rank = jnp.sum(
        (ahead & (question_of[None, :] == question_of[:, None])).astype(jnp.int32), axis=1
    )
    device_rank = jnp.sum(
        (ahead & (source_of[None, :] == source_of[:, None])).astype(jnp.int32), axis=1
    )
    gather_pick = jnp.sum(
        (
            on_segment[:, None, None, None, None]
            & (
                question_of[:, None, None, None, None]
                == jnp.arange(q_here, dtype=jnp.int32)[None, :, None, None, None]
            )
            & (
                segment_rank[:, None, None, None, None]
                == jnp.arange(per_segment, dtype=jnp.int32)[None, None, :, None, None]
            )
            & (
                source_of[:, None, None, None, None]
                == jnp.arange(columns, dtype=jnp.int32)[None, None, None, :, None]
            )
            & (
                device_rank[:, None, None, None, None]
                == jnp.arange(per_device, dtype=jnp.int32)[None, None, None, None, :]
            )
        ).astype(jnp.int32),
        axis=0,
    ).astype(jnp.bfloat16)
    compact = jnp.einsum(
        "krgc,gcsx->krsx", gather_pick, incoming, preferred_element_type=jnp.float32
    ).astype(jnp.bfloat16)
    pooled = lax.all_gather(compact[None], "segment", axis=0, tiled=True)
    segment_counts = jnp.sum(
        (
            row_live[None, None, :]
            & (question_of[None, None, :] == jnp.arange(q_here, dtype=jnp.int32)[:, None, None])
            & (segment_of[None, None, :] == jnp.arange(segments, dtype=jnp.int32)[None, :, None])
        ).astype(jnp.int32),
        axis=2,
    )
    live_slots = (
        jnp.arange(per_segment, dtype=jnp.int32)[None, None, :] < segment_counts[:, :, None]
    )
    key_total = segments * per_segment * seq_len
    key_live = (
        jnp.broadcast_to(live_slots[:, :, :, None], (q_here, segments, per_segment, seq_len))
        .reshape(q_here, key_total)
        .astype(jnp.float32)
    )

    def head_pass(head_no):
        first_col = head_no * HEAD_DIM
        key_head = lax.dynamic_slice_in_dim(pooled, first_col, HEAD_DIM, 4)
        value_head = lax.dynamic_slice_in_dim(pooled, inner_here + first_col, HEAD_DIM, 4)
        query_head = lax.dynamic_slice_in_dim(queries, first_col, HEAD_DIM, 2)
        grad_head = lax.dynamic_slice_in_dim(context_grad, first_col, HEAD_DIM, 2)
        scores = jnp.einsum(
            "ktd,skrld->ktsrl", query_head, key_head, preferred_element_type=jnp.float32
        )
        scores = scores.reshape(q_here, target_len, key_total) * scaling
        weights = jnp.exp(scores) * key_live[:, None, :]
        attn_probs = weights / jnp.sum(weights, axis=-1, keepdims=True)
        probs_half = attn_probs.astype(jnp.bfloat16).reshape(
            q_here, target_len, segments, per_segment, seq_len
        )
        context = jnp.einsum(
            "ktsrl,skrld->ktd", probs_half, value_head, preferred_element_type=jnp.float32
        ).astype(jnp.bfloat16)
        row_delta = jnp.sum(
            grad_head.astype(jnp.float32) * context.astype(jnp.float32), axis=-1, keepdims=True
        )
        prob_grads = jnp.einsum(
            "ktd,skrld->ktsrl", grad_head, value_head, preferred_element_type=jnp.float32
        )
        prob_grads = prob_grads.reshape(q_here, target_len, key_total)
        score_grads = (attn_probs * (prob_grads - row_delta)).astype(jnp.bfloat16)
        score_grads = score_grads.reshape(q_here, target_len, segments, per_segment, seq_len)
        score_mine = lax.dynamic_index_in_dim(score_grads, segment_at, 2, keepdims=False)
        probs_mine = lax.dynamic_index_in_dim(probs_half, segment_at, 2, keepdims=False)
        key_grads = (
            jnp.einsum("ktrl,ktd->krld", score_mine, query_head, preferred_element_type=jnp.float32)
            * scaling
        ).astype(jnp.bfloat16)
        value_grads = jnp.einsum(
            "ktrl,ktd->krld", probs_mine, grad_head, preferred_element_type=jnp.float32
        ).astype(jnp.bfloat16)
        return (key_grads, value_grads)

    key_grads, value_grads = lax.map(head_pass, jnp.arange(heads_here, dtype=jnp.int32))
    grad_shape = (q_here, per_segment, seq_len, inner_here)
    key_grads = jnp.moveaxis(key_grads, 0, 3).reshape(grad_shape)
    value_grads = jnp.moveaxis(value_grads, 0, 3).reshape(grad_shape)
    my_share = jnp.concatenate([key_grads, value_grads], axis=-1)
    spread_back = jnp.einsum(
        "krgc,krsx->gcsx", gather_pick, my_share, preferred_element_type=jnp.float32
    ).astype(jnp.bfloat16)
    owner_back = lax.all_to_all(spread_back, "dp", split_axis=0, concat_axis=0, tiled=True)
    token_grads = jnp.einsum(
        "gcl,gcsx->slx", send_pick, owner_back, preferred_element_type=jnp.float32
    ).astype(jnp.bfloat16)
    grad_flat = token_grads.reshape(row_count, 2 * inner_here)
    my_rows = row_count // tensor_ways
    token_share = seq_len // tensor_ways
    normed_grad = lax.psum_scatter(
        (
            project_back(grad_flat[:, :inner_here], key_full)
            + project_back(grad_flat[:, inner_here:], value_full)
        ).astype(jnp.bfloat16),
        "mp",
        scatter_dimension=0,
        tiled=True,
    ).astype(jnp.float32)
    first_token = tensor_at * token_share
    states_mine = lax.dynamic_slice_in_dim(hidden, first_token, token_share, 1).astype(jnp.float32)
    states_mine = states_mine.transpose(1, 0, 2).reshape(my_rows, model_width)
    rms_mine = lax.dynamic_slice_in_dim(
        inv_rms.reshape(slots_here, seq_len, 1), first_token, token_share, 1
    )
    rms_mine = rms_mine.transpose(1, 0, 2).reshape(my_rows, 1)
    scaled = gain_vec * normed_grad
    hidden_grad = rms_mine * scaled - states_mine * rms_mine**3 * jnp.mean(
        states_mine * scaled, axis=-1, keepdims=True
    )
    hidden_grad = hidden_grad.reshape(token_share, slots_here, model_width).transpose(1, 0, 2)
    return hidden_grad.astype(jnp.bfloat16)


def solution(mesh):
    in_specs = (
        P(("segment", "dp"), None, None),
        P(),
        P("dp", "mp"),
        P("dp", "mp"),
        P("dp", None, "mp"),
        P("dp", None, "mp"),
        P(),
        P(),
        P(),
    )
    out_specs = P(("segment", "dp"), "mp", None)
    return jax.shard_map(
        on_device, mesh=mesh, in_specs=in_specs, out_specs=out_specs, check_vma=False
    )
```

profile of v0, /device:TPU:1, one launch (start us, length us, event | category | flops | bytes accessed | tf_op | source)
XLA Modules:
  0.0 518.2 jit_solution(18247863727032568012)
XLA Ops:
  8.7 2.6 multiply_reduce_fusion
  13.1 2.7 fusion.34
  15.8 75.3 %all-gather.7.cloned.1.call-done = bf16[4096,512]{1,0:T(8,128)(2,1)} async-done(((bf16[256,512]{1,0:T(8,128)(2,1)}), bf16[4096,512]{1,0:T(8,128)(2,1)}) %all-gather.7.cloned.1.call-update) | async-done | bytes 4194320 | tf_op jit(solution)/shard_map/all_gather | solution.py:44
  91.1 4.9 convolution_convert_fusion.1
  96.0 82.6 %all-gather.5.cloned.1.call-done = bf16[4096,512]{1,0:T(8,128)(2,1)} async-done(((bf16[256,512]{1,0:T(8,128)(2,1)}), bf16[4096,512]{1,0:T(8,128)(2,1)}) %all-gather.5.cloned.1.call-update) | async-done | bytes 4194320 | tf_op jit(solution)/shard_map/all_gather | solution.py:43
  178.6 4.0 convolution_convert_fusion.2
  183.7 2.5 copy.68
  186.2 5.6 %all-to-all-start = ((bf16[16,1,64,1024]{3,2,1,0:T(8,128)(2,1)}), bf16[16,1,64,1024]{3,2,1,0:T(8,128)(2,1)S(1)}, u32[]{:S(2)}, u32[]{:S(2)}) async-start(bf16[16,1,64,1024]{3,2,1,0:T(8,128)(2,1)} %copy.68), calls=%async_computation | async-start | bytes 4194304 | tf_op jit(solution)/shard_map/all_to_all | solution.py:95
  193.4 35.5 %all-to-all-done = bf16[16,1,64,1024]{3,2,1,0:T(8,128)(2,1)S(1)} async-done(((bf16[16,1,64,1024]{3,2,1,0:T(8,128)(2,1)}), bf16[16,1,64,1024]{3,2,1,0:T(8,128)(2,1)S(1)}, u32[]{:S(2)}, u32[]{:S(2)}) %all-to-all-start) | async-done | bytes 2097184 | tf_op jit(solution)/shard_map/all_to_all | solution.py:95
  228.9 1.5 fusion.44
  230.5 2.0 copy.70
  233.4 99.8 %all-gather.9.cloned.1.call-done = bf16[8,6,64,1024]{3,2,1,0:T(8,128)(2,1)} async-done(((bf16[2,6,64,1024]{3,2,1,0:T(8,128)(2,1)}), bf16[8,6,64,1024]{3,2,1,0:T(8,128)(2,1)}) %all-gather.9.cloned.1.call-update) | async-done | bytes 6291472 | tf_op jit(solution)/shard_map/all_gather | solution.py:143
  333.2 6.7 %copy.72 = bf16[4,2,6,64,1024]{4,3,2,0,1:T(8,128)(2,1)} copy(bf16[4,2,6,64,1024]{4,3,2,1,0:T(8,128)(2,1)} %bitcast.142) | data formatting | bytes 12582912
  339.9 57.2 %while.15 = (s32[]{:T(128)}, bf16[8,2,6,64,64]{4,3,2,1,0:T(8,128)(2,1)}, bf16[8,2,6,64,64]{4,3,2,1,0:T(8,128)(2,1)}, s32[8]{0:T(128)S(1)}, bf16[2,128,512]{1,2,0...) while((s32[]{:T(128)}, ...), condition=%wide.region_16.17_spmd.clone, body=%wide.region_13.16_spmd.clone.sunk | while | flops 178650624 | bytes 12167454 | solution.py:200
  341.1 1.6 fusion.113
  348.2 1.6 fusion.113
  355.4 1.6 fusion.113
  362.5 1.6 fusion.113
  369.7 1.6 fusion.113
  376.9 1.6 fusion.113
  384.0 1.6 fusion.113
  391.1 1.6 fusion.113
  397.1 2.4 copy.90
  400.6 2.4 copy.91
  403.0 1.8 reshape.671
  404.8 2.4 fusion.47
  408.4 51.3 %all_to_all.10 = bf16[16,1,64,1024]{3,2,1,0:T(8,128)(2,1)S(1)} all-to-all(bf16[16,1,64,1024]{3,2,1,0:T(8,128)(2,1)S(1)} %copy.78), channel_id=1, replica_groups=mesh['segment'=4,'dp'=16,'mp'=4] {'dp'}, dimensions={0} | all-to-all | bytes 4194304 | tf_op jit(solution)/shard_map/all_to_all | solution.py:208
  461.3 4.2 fusion.58
  465.5 3.5 add_convert_fusion
  470.3 2.3 copy.80
  472.6 1.7 reshape.658
  474.6 33.6 %reduce-scatter.2.cloned.1.call-done = bf16[96,4096]{1,0:T(8,128)(2,1)} async-done(((bf16[384,4096]{1,0:T(8,128)(2,1)}), bf16[96,4096]{1,0:T(8,128)(2,1)}) %reduce-scatter.2.cloned.1.call-update) | async-done | bytes 786448 | tf_op jit(solution)/shard_map/reduce_scatter | solution.py:215
  (169 shorter events, 55.1 us)
Async XLA Ops:
  6.5 6.6 %copy-start = (bf16[6,64,4096]{2,1,0:T(8,128)(2,1)S(1)}, bf16[6,64,4096]{2,1,0:T(8,128)(2,1)}, u32[]{:S(2)}) copy-start(bf16[6,64,4096]{2,1,0:T(8,128)(2,1)} %param.11) | copy-start | bytes 9437188
  6.5 4.9 copy-start.21
  6.5 5.0 copy-start.6
  6.5 5.0 copy-start.20
  6.5 84.5 %all-gather.7.cloned.1.call-start = ((), (), s32[]{:S(2)}) async-start(), calls=%async_computation.4 | async-start | bytes 4456448 | tf_op jit(solution)/shard_map/all_gather | solution.py:44
  7.3 171.3 %all-gather.5.cloned.1.call-start = ((), (), s32[]{:S(2)}) async-start(), calls=%async_computation.3 | async-start | bytes 4456448 | tf_op jit(solution)/shard_map/all_gather | solution.py:43
  11.3 4.5 copy-start.8
  11.6 4.2 copy-start.10
  11.8 4.0 copy-start.12
  12.3 3.5 copy-start.15
  15.8 162.8 %copy-start.2 = (bf16[384,4096]{1,0:T(8,128)(2,1)S(1)}, bf16[384,4096]{1,0:T(8,128)(2,1)}, u32[]{:S(2)}) copy-start(bf16[384,4096]{1,0:T(8,128)(2,1)} %fusion.34) | copy-start | bytes 9437188
  178.6 4.1 copy-start.13
  178.6 4.1 copy-start.16
  178.6 4.1 copy-start.18
  186.2 5.7 %copy-start.22 = (s32[32]{0:T(128)S(1)}, s32[32]{0:T(128)}, u32[]{:S(2)}) copy-start(s32[32]{0:T(128)} %param.19) | copy-start | bytes 388
  186.2 6.0 %copy-start.7 = (s32[32,16]{0,1:T(8,128)S(1)}, s32[32,16]{0,1:T(8,128)}, u32[]{:S(2)}) copy-start(s32[32,16]{0,1:T(8,128)} %param.18) | copy-start | bytes 6148
  186.2 6.2 %copy-start.11 = (pred[32,16]{0,1:T(8,128)(4,1)S(1)}, pred[32,16]{0,1:T(8,128)(4,1)}, u32[]{:S(2)}) copy-start(pred[32,16]{0,1:T(8,128)(4,1)} %copy-done.10) | copy-start | bytes 1540
  186.2 42.8 %all-to-all-start = ((bf16[16,1,64,1024]{3,2,1,0:T(8,128)(2,1)}), bf16[16,1,64,1024]{3,2,1,0:T(8,128)(2,1)S(1)}, u32[]{:S(2)}, u32[]{:S(2)}) async-start(bf16[16,1,64,1024]{3,2,1,0:T(8,128)(2,1)} %copy.68), calls=%async_computation | async-start | bytes 4194304 | tf_op jit(solution)/shard_map/all_to_all | solution.py:95
  191.8 141.4 %all-gather.9.cloned.1.call-start = ((), (), s32[]{:S(2)}) async-start(), calls=%async_computation.6 | async-start | bytes 7864320 | tf_op jit(solution)/shard_map/all_gather | solution.py:143
  230.5 2.3 copy-start.4
  230.5 2.5 copy-start.5
  232.5 275.6 %reduce-scatter.2.cloned.1.call-start = ((), (), s32[]{:S(2)}) async-start(), calls=%async_computation.5 | async-start | bytes 3932160 | tf_op jit(solution)/shard_map/reduce_scatter | solution.py:215
  408.4 51.3 %copy-start.14 = (pred[6]{0:T(512)(128)(4,1)S(1)}, pred[6]{0:T(512)(128)(4,1)}, u32[]{:S(2)}) copy-start(pred[6]{0:T(512)(128)(4,1)} %copy-done.12) | copy-start | bytes 22
  408.4 51.3 %copy-start.17 = (s32[6]{0:T(128)S(1)}, s32[6]{0:T(128)}, u32[]{:S(2)}) copy-start(s32[6]{0:T(128)} %copy-done.15) | copy-start | bytes 76
  408.4 51.3 %copy-start.19 = (pred[6]{0:T(512)(128)(4,1)S(1)}, pred[6]{0:T(512)(128)(4,1)}, u32[]{:S(2)}) copy-start(pred[6]{0:T(512)(128)(4,1)} %broadcast_compare_fusion) | copy-start | bytes 22
  461.3 4.2 copy-start.1
  472.6 1.7 copy-start.9
  508.1 1.5 copy-start.3
Sparse Core Ops, SparseCore 0:
  9.1 81.8 all-gather.6
  92.9 85.7 all-gather.4
  232.7 100.5 all-gather.8
  469.1 38.9 reduce-scatter.1
where the time goes:
time: 519 us; the launch traced here: 518 us
  waiting for transfers between devices  328 us (63%)
  matrix products  56.4 us (11%)
  blocking collectives  51.3 us (10%)
  local copies, waits for them, and re-layouts  43.2 us (8%)
  other arithmetic  14.6 us (3%)
  between operations  13.6 us (3%)
  starting transfers between devices  5.98 us (1%)
    all_gather x1, waiting for transfers between devices, on_device(): pooled = lax.all_gather(compact[None], 'segment', axis=0, tiled=True)  99.8 us
    all_gather x1, waiting for transfers between devices, on_device(): lax.all_gather(key_weight, 'dp', axis=0, tiled=True)  82.6 us
    all_gather x1, waiting for transfers between devices, on_device(): lax.all_gather(value_weight, 'dp', axis=0, tiled=True)  75.3 us
    all_to_all x1, blocking collectives, on_device(): lax.all_to_all(spread_back, 'dp', split_axis=0, concat_axis=0, tiled=True)  51.3 us
    all_to_all x1, waiting for transfers between devices, on_device(): lax.all_to_all(outgoing, 'dp', split_axis=0, concat_axis=0, tiled=True)  35.5 us
    reduce_scatter x1, waiting for transfers between devices, on_device(): lax.psum_scatter((project_back(grad_flat[:, :inner_here], key_full) + pro...  33.6 us
    dot_general x8, matrix products, head_pass(): jnp.einsum('ktd,skrld->ktsrl', query_head, key_head, preferred_element_ty...  13.2 us
    dynamic_slice x8, local copies, waits for them, and re-layouts, head_pass(): lax.dynamic_slice_in_dim(pooled, inner_here + first_col, HEAD_DIM, 4)  11.4 us
  transfers between devices with their start and end apart: 5, of which 5 were waited for; matrix products, arithmetic and copies ran while one was open for 4% of the time, Pallas kernels for 0%

commit v1 on v0

--- a/solution.py
+++ b/solution.py
@@ -19,6 +19,19 @@
     passage_slot,
     slot_question,
 ):
+
+    def _search_stops_all(message, device_axis):
+        current_value = jnp.concatenate(
+            lax.all_to_all(
+                jnp.stack([message for _ in range(lax.axis_size(device_axis))]),
+                axis_name=device_axis,
+                split_axis=0,
+                concat_axis=0,
+            ),
+            axis=0,
+        )
+        return current_value
+
     segments = lax.axis_size("segment")
     columns = lax.axis_size("dp")
     tensor_ways = lax.axis_size("mp")
@@ -41,7 +54,7 @@
     scaling = 1.0 / math.sqrt(HEAD_DIM)
     key_full, value_full = (
         lax.all_gather(key_weight, "dp", axis=0, tiled=True),
-        lax.all_gather(value_weight, "dp", axis=0, tiled=True),
+        _search_stops_all(value_weight, "dp"),
     )
 
     def project(normed_rows, weight_full):

time: 519 us -> 504 us (0.971)
  waiting for transfers between devices: 328 us -> 281 us
  starting transfers between devices: 5.98 us -> 31.4 us
    all_to_all x0 -> x1, waiting for transfers between devices: none -> 108 us  [_search_stops_all(): lax.all_to_all(jnp.stack([message for _ in range(lax.axis_size(device_axi...]
    all_gather x1, waiting for transfers between devices: 82.6 us -> 2.12 us  [on_device(): lax.all_gather(key_weight, 'dp', axis=0, tiled=True)]
    all_gather x1 -> x0, waiting for transfers between devices: 75.3 us -> none  [on_device(): lax.all_gather(value_weight, 'dp', axis=0, tiled=True)]
    all_to_all x1, starting transfers between devices: 5.65 us -> 21.6 us  [on_device(): lax.all_to_all(outgoing, 'dp', split_axis=0, concat_axis=0, tiled=True)]
    all_to_all x0 -> x1, starting transfers between devices: none -> 9.49 us  [_search_stops_all(): lax.all_to_all(jnp.stack([message for _ in range(lax.axis_size(device_axi...]
where the time goes in v1:
time: 504 us; the launch traced here: 502 us
  waiting for transfers between devices  281 us (56%)
  matrix products  58.6 us (12%)
  blocking collectives  51.3 us (10%)
  local copies, waits for them, and re-layouts  46.9 us (9%)
  starting transfers between devices  31.4 us (6%)
  other arithmetic  14.8 us (3%)
  between operations  13.6 us (3%)
    all_to_all x1, waiting for transfers between devices, _search_stops_all(): lax.all_to_all(jnp.stack([message for _ in range(lax.axis_size(device_axi...  108 us
    all_gather x1, waiting for transfers between devices, on_device(): pooled = lax.all_gather(compact[None], 'segment', axis=0, tiled=True)  96.5 us
    all_to_all x1, blocking collectives, on_device(): lax.all_to_all(spread_back, 'dp', split_axis=0, concat_axis=0, tiled=True)  51.3 us
    all_to_all x1, waiting for transfers between devices, on_device(): lax.all_to_all(outgoing, 'dp', split_axis=0, concat_axis=0, tiled=True)  39.9 us
    reduce_scatter x1, waiting for transfers between devices, on_device(): lax.psum_scatter((project_back(grad_flat[:, :inner_here], key_full) + pro...  33.6 us
    all_to_all x1, starting transfers between devices, on_device(): lax.all_to_all(outgoing, 'dp', split_axis=0, concat_axis=0, tiled=True)  21.6 us
    dot_general x8, matrix products, head_pass(): jnp.einsum('ktd,skrld->ktsrl', query_head, key_head, preferred_element_ty...  13.2 us
    dynamic_slice x8, local copies, waits for them, and re-layouts, head_pass(): lax.dynamic_slice_in_dim(pooled, inner_here + first_col, HEAD_DIM, 4)  11.4 us
  transfers between devices with their start and end apart: 5, of which 5 were waited for; matrix products, arithmetic and copies ran while one was open for 4% of the time, Pallas kernels for 0%

profile of v1, /device:TPU:1, one launch (start us, length us, event | category | flops | bytes accessed | tf_op | source)
XLA Modules:
  0.0 502.3 jit_solution(12956226049567279889)
XLA Ops:
  6.5 3.3 stack.2
  9.8 9.5 %all-to-all-start = ((bf16[16,256,512]{2,1,0:T(8,128)(2,1)}), bf16[16,256,512]{2,1,0:T(8,128)(2,1)}, u32[]{:S(2)}, u32[]{:S(2)}) async-start(bf16[16,256,512]{2,1,0:T(8,128)(2,1)} %stack.2), calls=%async_computation | async-start | bytes 8388608 | tf_op jit(solution)/shard_map/all_to_all | solution.py:25
  23.0 2.7 fusion.34
  25.7 2.7 multiply_convert_fusion
  28.5 107.9 %all-to-all-done = bf16[16,256,512]{2,1,0:T(8,128)(2,1)} async-done(((bf16[16,256,512]{2,1,0:T(8,128)(2,1)}), bf16[16,256,512]{2,1,0:T(8,128)(2,1)}, u32[]{:S(2)}, u32[]{:S(2)}) %all-to-all-start) | async-done | bytes 4194336 | tf_op jit(solution)/shard_map/all_to_all | solution.py:25
  136.3 5.1 %convolution_convert_fusion.1 = bf16[384,512]{1,0:T(8,128)(2,1)S(1)} fusion(bf16[384,4096]{1,0:T(8,128)(2,1)} %bitcast.147, bf16[4096,512]{1,0:T(8,128)(2,1)} %bitcast.8), kind=kOutput, calls=%fused_computation.64 | convolution fusion | flops 1610809344 | bytes 7733248 | tf_op jit(solution)/shard_map/dot_general | solution.py:61
  141.5 2.1 all-gather.4.cloned.1.call-done
  143.6 4.0 convolution_convert_fusion.2
  148.6 2.5 copy.68
  151.1 21.6 %all-to-all-start.1 = ((bf16[16,1,64,1024]{3,2,1,0:T(8,128)(2,1)}), bf16[16,1,64,1024]{3,2,1,0:T(8,128)(2,1)S(1)}, u32[]{:S(2)}, u32[]{:S(2)}) async-start(bf16[16,1,64,1024]{3,2,1,0:T(8,128)(2,1)} %copy.68), calls=%async_computation.1 | async-start | bytes 4194304 | tf_op jit(solution)/shard_map/all_to_all | solution.py:108
  174.4 39.9 %all-to-all-done.1 = bf16[16,1,64,1024]{3,2,1,0:T(8,128)(2,1)S(1)} async-done(((bf16[16,1,64,1024]{3,2,1,0:T(8,128)(2,1)}), bf16[16,1,64,1024]{3,2,1,0:T(8,128)(2,1)S(1)}, u32[]{:S(2)}, u32[]{:S(2)}) %all-to-all-start.1) | async-done | bytes 2097184 | tf_op jit(solution)/shard_map/all_to_all | solution.py:108
  215.9 2.0 copy.70
  218.8 96.5 %all-gather.6.cloned.1.call-done = bf16[8,6,64,1024]{3,2,1,0:T(8,128)(2,1)} async-done(((bf16[2,6,64,1024]{3,2,1,0:T(8,128)(2,1)}), bf16[8,6,64,1024]{3,2,1,0:T(8,128)(2,1)}) %all-gather.6.cloned.1.call-update) | async-done | bytes 6291472 | tf_op jit(solution)/shard_map/all_gather | solution.py:156
  315.2 6.7 %copy.72 = bf16[4,2,6,64,1024]{4,3,2,0,1:T(8,128)(2,1)} copy(bf16[4,2,6,64,1024]{4,3,2,1,0:T(8,128)(2,1)} %bitcast.144) | data formatting | bytes 12582912
  321.9 57.2 %while.15 = (s32[]{:T(128)}, bf16[8,2,6,64,64]{4,3,2,1,0:T(8,128)(2,1)}, bf16[8,2,6,64,64]{4,3,2,1,0:T(8,128)(2,1)}, s32[8]{0:T(128)S(1)}, bf16[2,128,512]{1,2,0...) while((s32[]{:T(128)}, ...), condition=%wide.region_16.17_spmd.clone, body=%wide.region_13.16_spmd.clone.sunk | while | flops 178650624 | bytes 12167454 | solution.py:213
  330.3 1.6 fusion.113
  337.4 1.6 fusion.113
  344.6 1.6 fusion.113
  351.7 1.6 fusion.113
  358.9 1.6 fusion.113
  366.0 1.6 fusion.113
  373.2 1.6 fusion.113
  379.2 2.4 copy.90
  382.6 2.4 copy.91
  385.1 1.8 reshape.687
  386.9 2.4 fusion.47
  390.5 51.3 %all_to_all.15 = bf16[16,1,64,1024]{3,2,1,0:T(8,128)(2,1)S(1)} all-to-all(bf16[16,1,64,1024]{3,2,1,0:T(8,128)(2,1)S(1)} %copy.78), channel_id=1, replica_groups=mesh['segment'=4,'dp'=16,'mp'=4] {'dp'}, dimensions={0} | all-to-all | bytes 4194304 | tf_op jit(solution)/shard_map/all_to_all | solution.py:221
  443.3 4.0 fusion.58
  447.4 5.7 %add_convert_fusion = bf16[384,4096]{1,0:T(8,128)(2,1)} fusion(f32[384,4096]{1,0:T(8,128)S(1)} %fusion.58, bf16[4096,512]{1,0:T(8,128)(2,1)} %bitcast.8, bf16[384,1024]{1,0:T(8,128)(2,1)S(1)} %reshape.669), kind=kOutput, calls=%fused_computation.42 | convolution fusion | flops 1613758464 | bytes 14024704 | tf_op jit(solution)/shard_map/dot_general | solution.py:64
  454.4 2.3 copy.80
  456.7 1.7 reshape.674
  458.6 33.6 %reduce-scatter.2.cloned.1.call-done = bf16[96,4096]{1,0:T(8,128)(2,1)} async-done(((bf16[384,4096]{1,0:T(8,128)(2,1)}), bf16[96,4096]{1,0:T(8,128)(2,1)}) %reduce-scatter.2.cloned.1.call-update) | async-done | bytes 786448 | tf_op jit(solution)/shard_map/reduce_scatter | solution.py:228
  (170 shorter events, 58.0 us)
Async XLA Ops:
  9.8 10.3 %copy-start.17 = (bf16[4096]{0:T(1024)(128)(2,1)S(1)}, bf16[4096]{0:T(1024)(128)(2,1)}, u32[]{:S(2)}) copy-start(bf16[4096]{0:T(1024)(128)(2,1)} %param.12) | copy-start | bytes 24580
  9.8 10.3 %copy-start = (bf16[6,64,4096]{2,1,0:T(8,128)(2,1)S(1)}, bf16[6,64,4096]{2,1,0:T(8,128)(2,1)}, u32[]{:S(2)}) copy-start(bf16[6,64,4096]{2,1,0:T(8,128)(2,1)} %param.11) | copy-start | bytes 9437188
  9.8 126.5 %all-to-all-start = ((bf16[16,256,512]{2,1,0:T(8,128)(2,1)}), bf16[16,256,512]{2,1,0:T(8,128)(2,1)}, u32[]{:S(2)}, u32[]{:S(2)}) async-start(bf16[16,256,512]{2,1,0:T(8,128)(2,1)} %stack.2), calls=%async_computation | async-start | bytes 8388608 | tf_op jit(solution)/shard_map/all_to_all | solution.py:25
  19.3 1.6 copy-start.21
  19.3 1.7 copy-start.5
  19.3 1.7 copy-start.20
  19.4 124.2 %all-gather.4.cloned.1.call-start = ((), (), s32[]{:S(2)}) async-start(), calls=%async_computation.4 | async-start | bytes 4456448 | tf_op jit(solution)/shard_map/all_gather | solution.py:56
  20.8 4.9 copy-start.7
  21.1 0.6 copy-start.9
  21.3 0.6 copy-start.11
  21.9 0.5 copy-start.14
  136.3 7.3 %copy-start.1 = (bf16[384,4096]{1,0:T(8,128)(2,1)S(1)}, bf16[384,4096]{1,0:T(8,128)(2,1)}, u32[]{:S(2)}) copy-start(bf16[384,4096]{1,0:T(8,128)(2,1)} %fusion.34) | copy-start | bytes 9437188
  143.6 4.1 copy-start.12
  143.6 4.1 copy-start.15
  143.6 4.1 copy-start.18
  151.1 21.7 %copy-start.22 = (s32[32]{0:T(128)S(1)}, s32[32]{0:T(128)}, u32[]{:S(2)}) copy-start(s32[32]{0:T(128)} %param.19) | copy-start | bytes 388
  151.1 22.0 %copy-start.6 = (s32[32,16]{0,1:T(8,128)S(1)}, s32[32,16]{0,1:T(8,128)}, u32[]{:S(2)}) copy-start(s32[32,16]{0,1:T(8,128)} %param.18) | copy-start | bytes 6148
  151.1 22.2 %copy-start.10 = (pred[32,16]{0,1:T(8,128)(4,1)S(1)}, pred[32,16]{0,1:T(8,128)(4,1)}, u32[]{:S(2)}) copy-start(pred[32,16]{0,1:T(8,128)(4,1)} %copy-done.9) | copy-start | bytes 1540
  151.1 63.2 %all-to-all-start.1 = ((bf16[16,1,64,1024]{3,2,1,0:T(8,128)(2,1)}), bf16[16,1,64,1024]{3,2,1,0:T(8,128)(2,1)S(1)}, u32[]{:S(2)}, u32[]{:S(2)}) async-start(bf16[16,1,64,1024]{3,2,1,0:T(8,128)(2,1)} %copy.68), calls=%async_computation.1 | async-start | bytes 4194304 | tf_op jit(solution)/shard_map/all_to_all | solution.py:108
  172.8 142.4 %all-gather.6.cloned.1.call-start = ((), (), s32[]{:S(2)}) async-start(), calls=%async_computation.6 | async-start | bytes 7864320 | tf_op jit(solution)/shard_map/all_gather | solution.py:156
  215.8 2.3 copy-start.3
  215.9 2.5 copy-start.4
  217.9 274.3 %reduce-scatter.2.cloned.1.call-start = ((), (), s32[]{:S(2)}) async-start(), calls=%async_computation.5 | async-start | bytes 3932160 | tf_op jit(solution)/shard_map/reduce_scatter | solution.py:228
  390.4 51.3 %copy-start.13 = (pred[6]{0:T(512)(128)(4,1)S(1)}, pred[6]{0:T(512)(128)(4,1)}, u32[]{:S(2)}) copy-start(pred[6]{0:T(512)(128)(4,1)} %copy-done.11) | copy-start | bytes 22
  390.5 51.3 %copy-start.16 = (s32[6]{0:T(128)S(1)}, s32[6]{0:T(128)}, u32[]{:S(2)}) copy-start(s32[6]{0:T(128)} %copy-done.14) | copy-start | bytes 76
  390.5 51.3 %copy-start.19 = (pred[6]{0:T(512)(128)(4,1)S(1)}, pred[6]{0:T(512)(128)(4,1)}, u32[]{:S(2)}) copy-start(pred[6]{0:T(512)(128)(4,1)} %broadcast_compare_fusion) | copy-start | bytes 22
  456.7 1.7 copy-start.8
  492.2 1.5 copy-start.2
Sparse Core Ops, SparseCore 0:
  22.0 121.5 all-gather.3
  218.0 97.1 all-gather.5
  453.2 38.9 reduce-scatter.1
